TPU v7x, 128 devices: a whole 4x4x4 slice. The times are simulated.
128 devices in a mesh: expert: 32 (over z, x, core), etp: 4 (over y).
Axes of the slice: x: 4, y: 4, z: 4, core: 2. Of those that a mesh axis runs over, the one named last changes fastest.
Arguments:
- tokens: bfloat16 [16384, 2560], P(('expert', 'etp')), may hold values from -6 to 6
- routes: int32 [16384, 1], P(('expert', 'etp')), may hold values from 0 to 31; in each aligned block of 128 rows (0 to 127, 128 to 255, ...) at most 12 rows name the same one
- scores: float32 [16384], P(('expert', 'etp')), may hold values from 0.1 to 1
- gate_weight: bfloat16 [32, 2560, 4096], P('expert', None, 'etp'), may hold values from -0.125 to 0.125
- up_weight: bfloat16 [32, 2560, 4096], P('expert', None, 'etp'), may hold values from -0.125 to 0.125
- down_weight: bfloat16 [32, 4096, 2560], P('expert', 'etp'), may hold values from -0.09375 to 0.09375
Outputs:
- layer_out: bfloat16 [16384, 2560], P(('expert', 'etp'))
Inputs may be any that keep to these rules, and one draw needn't show every extreme that they name: `routes`: within each device's aligned block of 128 rows no expert is named by more than 12 rows, a bound that some block reaches; every expert is named by some row.
All inputs are finite; a program needn't handle non-finite values.
Results may differ from a plain program's by a relative error of at most 0.014.
Values may be sent and summed in bfloat16 or wider, within the bound.
A program may use at most 128 MiB of HBM per device.

v0:
```python
import jax
import jax.numpy as jnp
from jax import lax
from jax.sharding import PartitionSpec as P


def hidden_rows(row_block, gate_local, up_local):
    flattened = row_block.reshape(-1, row_block.shape[-1])
    gate_out = jnp.dot(flattened, gate_local, preferred_element_type=jnp.float32)
    up_out = jnp.dot(flattened, up_local, preferred_element_type=jnp.float32)
    hidden = (jax.nn.silu(gate_out) * up_out).astype(jnp.bfloat16)
    return hidden.reshape(row_block.shape[:-1] + (gate_local.shape[1],))


def local(tokens, routes, scores, gate_weight, up_weight, down_weight):
    experts = lax.axis_size("expert")
    groups = lax.axis_size("etp")
    tok_rows, features = tokens.shape
    slot_count = 3 * tok_rows // experts
    expert_ids = routes[:, 0]
    onehot = (expert_ids[:, None] == jnp.arange(experts, dtype=jnp.int32)[None, :]).astype(
        jnp.int32
    )
    position = jnp.sum(
        (jnp.cumsum(onehot, axis=0, dtype=jnp.int32) - 1) * onehot, axis=1, dtype=jnp.int32
    )
    target = expert_ids * slot_count + position
    placing = (
        target[None, :] == jnp.arange(experts * slot_count, dtype=jnp.int32)[:, None]
    ).astype(jnp.bfloat16)
    outgoing = jnp.dot(placing, tokens, preferred_element_type=jnp.float32).astype(jnp.bfloat16)
    outgoing = outgoing.reshape(experts, slot_count, features)
    gate_local = gate_weight[0]
    up_local = up_weight[0]
    down_local = down_weight[0]
    grouped = lax.all_gather(outgoing, "etp", axis=1, tiled=True)
    received = lax.all_to_all(grouped, "expert", split_axis=0, concat_axis=0, tiled=True)
    hidden = hidden_rows(received, gate_local, up_local)
    partial_value = jnp.dot(
        hidden.reshape(-1, hidden.shape[-1]), down_local, preferred_element_type=jnp.float32
    )
    partial_value = partial_value.astype(jnp.bfloat16).reshape(
        experts, groups * slot_count, features
    )
    returned = lax.all_to_all(partial_value, "expert", split_axis=0, concat_axis=0, tiled=True)
    summed = lax.psum_scatter(
        returned.astype(jnp.float32).astype(jnp.bfloat16), "etp", scatter_dimension=1, tiled=True
    )
    collected = lax.dot_general(
        placing,
        summed.reshape(experts * slot_count, features),
        (((0,), (0,)), ((), ())),
        preferred_element_type=jnp.float32,
    )
    return (collected * scores[:, None]).astype(jnp.bfloat16)


def solution(mesh):
    in_specs = (
        P(("expert", "etp"), None),
        P(("expert", "etp"), None),
        P(("expert", "etp")),
        P("expert", None, "etp"),
        P("expert", None, "etp"),
        P("expert", "etp", None),
    )
    out_specs = P(("expert", "etp"), None)
    return jax.shard_map(local, mesh=mesh, in_specs=in_specs, out_specs=out_specs, check_vma=False)
```

profile of v0, /device:TPU:1, one launch (start us, length us, event | category | flops | bytes accessed | tf_op | source)
XLA Modules:
  0.0 436.1 jit_solution(5345934778175982684)
XLA Ops:
  6.5 0.8 fusion.13
  7.3 0.2 reduce_window_sum.11
  7.5 0.8 select_reduce_fusion
  8.3 0.7 multiply_add_fusion
  9.0 1.9 convolution_convert_fusion.1
  11.0 2.5 reshape.21
  13.5 2.5 copy.14
  15.9 0.0 all-gather.2.cloned.1.call-update
  15.9 0.0 reduce-scatter.2.cloned.1.call-start
  16.0 82.1 %all-gather.2.cloned.1.call-done = bf16[32,48,2560]{2,0,1:T(8,128)(2,1)} async-done(((bf16[32,12,2560]{2,0,1:T(8,128)(2,1)}), bf16[32,48,2560]{2,0,1:T(8,128)(2,1)}) %all-gather.2.cloned.1.call-update) | async-done | bytes 7864336 | tf_op jit(solution)/shard_map/all_gather | solution.py:36
  98.1 7.5 %copy.15 = bf16[32,48,2560]{2,1,0:T(8,128)(2,1)S(1)} copy(bf16[32,48,2560]{2,0,1:T(8,128)(2,1)} %all-gather.2.cloned.1.call-done) | data formatting | bytes 15728640 | tf_op jit(solution)/shard_map/all_gather | solution.py:36
  105.6 97.7 %all_to_all.10 = bf16[32,48,2560]{2,1,0:T(8,128)(2,1)S(1)} all-to-all(bf16[32,48,2560]{2,1,0:T(8,128)(2,1)S(1)} %copy.15), channel_id=1, replica_groups=mesh['expert'=32,'etp'=4] {'expert'}, dimensions={0} | all-to-all | bytes 15728640 | tf_op jit(solution)/shard_map/all_to_all | solution.py:37
  203.3 3.1 copy-done.2
  206.4 12.3 %fusion.1 = f32[1536,1024]{1,0:T(8,128)} fusion(bf16[1536,2560]{1,0:T(8,128)(2,1)S(1)} %bitcast.21, bf16[1,2560,1024]{2,1,0:T(8,128)(2,1)} %param.10), kind=kOutput, calls=%fused_computation.3 | convolution fusion | flops 8053063680 | bytes 19398656 | tf_op jit(solution)/shard_map/dot_general | solution.py:10
  218.7 25.3 %convolution_convert_fusion = bf16[1536,2560]{1,0:T(8,128)(2,1)} fusion(bf16[1,1024,2560]{2,1,0:T(8,128)(2,1)} %param.11, f32[1536,1024]{1,0:T(8,128)} %fusion.1, bf16[1536,2560]{1,0:T(8,128)(2,1)} %bitcast.22, bf16[1,2560,1024]{2,1,0:T(8,128)(2,1)} %param.9), kind=kOutput, calls=%fused_computation | convolution fusion | flops 16119496704 | bytes 32505856 | tf_op jit(solution)/shard_map/dot_general | solution.py:39
  244.0 95.1 %all_to_all.11 = bf16[32,48,2560]{2,1,0:T(8,128)(2,1)S(1)} all-to-all(bf16[32,48,2560]{2,1,0:T(8,128)(2,1)} %bitcast.23), channel_id=1, replica_groups=mesh['expert'=32,'etp'=4] {'expert'}, dimensions={0} | all-to-all | bytes 15728640 | tf_op jit(solution)/shard_map/all_to_all | solution.py:45
  339.1 7.4 %copy.16 = bf16[32,48,2560]{2,0,1:T(8,128)(2,1)} copy(bf16[32,48,2560]{2,1,0:T(8,128)(2,1)S(1)} %all_to_all.11) | data formatting | bytes 15728640 | tf_op jit(solution)/shard_map/all_to_all | solution.py:45
  346.5 0.0 reduce-scatter.2.cloned.1.call-update
  346.5 0.0 copy-start.3
  346.5 0.0 copy-start.1
  346.6 75.1 %reduce-scatter.2.cloned.1.call-done = bf16[32,12,2560]{2,0,1:T(8,128)(2,1)} async-done(((bf16[32,48,2560]{2,0,1:T(8,128)(2,1)}), bf16[32,12,2560]{2,0,1:T(8,128)(2,1)}) %reduce-scatter.2.cloned.1.call-update) | async-done | bytes 1966096 | tf_op jit(solution)/shard_map/reduce_scatter | solution.py:46
  421.7 2.7 copy.17
  424.3 2.0 reshape.24
  426.4 2.9 fusion.9
  (6 shorter events, 0.0 us)
Async XLA Ops:
  6.5 2.5 copy-start
  6.5 91.5 %all-gather.2.cloned.1.call-start = ((), (), s32[]{:S(2)}) async-start(), calls=%async_computation.3 | async-start | bytes 9830400 | tf_op jit(solution)/shard_map/all_gather | solution.py:36
  15.9 405.7 %reduce-scatter.2.cloned.1.call-start = ((), (), s32[]{:S(2)}) async-start(), calls=%async_computation.4 | async-start | bytes 9830400 | tf_op jit(solution)/shard_map/reduce_scatter | solution.py:46
  203.3 3.1 copy-start.2
  346.5 79.8 %copy-start.3 = (f32[128]{0:T(128)S(1)}, f32[128]{0:T(128)}, u32[]{:S(2)}) copy-start(f32[128]{0:T(128)} %param.8) | copy-start | bytes 1540
  346.5 82.7 %copy-start.1 = (bf16[128,2560]{1,0:T(8,128)(2,1)S(1)}, bf16[128,2560]{1,0:T(8,128)(2,1)}, u32[]{:S(2)}) copy-start(bf16[128,2560]{1,0:T(8,128)(2,1)} %param.6) | copy-start | bytes 1966084
Sparse Core Ops, SparseCore 0:
  16.1 81.9 all-gather.1
  346.7 74.9 reduce-scatter.1
where the time goes:
time: 437 us; the launch traced here: 436 us
  blocking collectives  193 us (44%)
  waiting for transfers between devices  157 us (36%)
  matrix products  42.5 us (10%)
  local copies, waits for them, and re-layouts  27.6 us (6%)
  between operations  13.5 us (3%)
    all_to_all x1, blocking collectives, local(): lax.all_to_all(grouped, 'expert', split_axis=0, concat_axis=0, tiled=True)  97.7 us
    all_to_all x1, blocking collectives, local(): lax.all_to_all(partial_value, 'expert', split_axis=0, concat_axis=0, tile...  95.1 us
    all_gather x1, waiting for transfers between devices, local(): grouped = lax.all_gather(outgoing, 'etp', axis=1, tiled=True)  82.1 us
    reduce_scatter x1, waiting for transfers between devices, local(): lax.psum_scatter(returned.astype(jnp.float32).astype(jnp.bfloat16), 'etp'...  75.1 us
    dot_general x1, matrix products, local(): jnp.dot(hidden.reshape(-1, hidden.shape[-1]), down_local, preferred_eleme...  25.3 us
    dot_general x1, matrix products, hidden_rows(): up_out = jnp.dot(flattened, up_local, preferred_element_type=jnp.float32)  12.3 us
  transfers between devices with their start and end apart: 2, of which 2 were waited for; matrix products, arithmetic and copies ran while one was open for 0% of the time, Pallas kernels for 0%

commit v1 on v0

--- a/solution.py
+++ b/solution.py
@@ -33,7 +33,9 @@
     gate_local = gate_weight[0]
     up_local = up_weight[0]
     down_local = down_weight[0]
-    grouped = lax.all_gather(outgoing, "etp", axis=1, tiled=True)
+    grouped = jnp.concatenate(
+        lax.all_to_all(jnp.stack([outgoing] * lax.axis_size("etp")), "etp", 0, 0), axis=1
+    )
     received = lax.all_to_all(grouped, "expert", split_axis=0, concat_axis=0, tiled=True)
     hidden = hidden_rows(received, gate_local, up_local)
     partial_value = jnp.dot(

time: 437 us -> 445 us (1.018)
  blocking collectives: 193 us -> 287 us
  waiting for transfers between devices: 157 us -> 73.7 us
    all_to_all x0 -> x1, blocking collectives: none -> 92 us  [local(): lax.all_to_all(jnp.stack([outgoing] * lax.axis_size('etp')), 'etp', 0, 0)]
    all_gather x1 -> x0, waiting for transfers between devices: 82.1 us -> none  [local(): grouped = lax.all_gather(outgoing, 'etp', axis=1, tiled=True)]
    all_gather x1 -> x0, local copies, waits for them, and re-layouts: 7.54 us -> none  [local(): grouped = lax.all_gather(outgoing, 'etp', axis=1, tiled=True)]
    another operation x0 -> x3, local copies, waits for them, and re-layouts: none -> 4.48 us  [local(): jnp.stack([outgoing] * lax.axis_size('etp'))]
  transfers between devices with their start and end apart: 2 -> 1, of which waited for: 2 -> 1; matrix products, arithmetic and copies ran while one was open for 0% -> 0% of each run, Pallas kernels for 0% -> 0%
where the time goes in v1:
time: 445 us; the launch traced here: 444 us
  blocking collectives  287 us (64%)
  waiting for transfers between devices  73.7 us (17%)
  matrix products  40.3 us (9%)
  local copies, waits for them, and re-layouts  27 us (6%)
  between operations  13.5 us (3%)
    all_to_all x1, blocking collectives, local(): lax.all_to_all(grouped, 'expert', split_axis=0, concat_axis=0, tiled=True)  100 us
    all_to_all x1, blocking collectives, local(): lax.all_to_all(partial_value, 'expert', split_axis=0, concat_axis=0, tile...  95.1 us
    all_to_all x1, blocking collectives, local(): lax.all_to_all(jnp.stack([outgoing] * lax.axis_size('etp')), 'etp', 0, 0)  92 us
    reduce_scatter x1, waiting for transfers between devices, local(): lax.psum_scatter(returned.astype(jnp.float32).astype(jnp.bfloat16), 'etp'...  73.7 us
    dot_general x1, matrix products, local(): jnp.dot(hidden.reshape(-1, hidden.shape[-1]), down_local, preferred_eleme...  25.3 us
    dot_general x1, matrix products, hidden_rows(): up_out = jnp.dot(flattened, up_local, preferred_element_type=jnp.float32)  10.1 us
  transfers between devices with their start and end apart: 1, of which 1 were waited for; matrix products, arithmetic and copies ran while one was open for 0% of the time, Pallas kernels for 0%

profile of v1, /device:TPU:1, one launch (start us, length us, event | category | flops | bytes accessed | tf_op | source)
XLA Modules:
  0.0 444.4 jit_solution(11543738985774477868)
XLA Ops:
  6.5 0.0 copy-start
  6.5 0.8 fusion.13
  7.3 0.2 reduce_window_sum.11
  7.5 0.8 select_reduce_fusion
  8.3 0.7 multiply_add_fusion
  9.0 2.0 convolution_convert_fusion.1
  11.0 2.5 stack_reshape.2
  13.5 1.1 copy.14
  14.6 0.9 stack.3
  15.5 92.0 %all_to_all.15 = bf16[4,32,12,2560]{3,1,2,0:T(8,128)(2,1)S(1)} all-to-all(bf16[4,32,12,2560]{3,1,2,0:T(8,128)(2,1)S(1)} %stack.3), channel_id=1, replica_groups=mesh['expert'=32,'etp'=4] {'etp'}, dimensions={0} | all-to-all | bytes 15728640 | tf_op jit(solution)/shard_map/all_to_all | solution.py:37
  107.5 7.4 %copy.15 = bf16[32,48,2560]{2,1,0:T(8,128)(2,1)} copy(bf16[32,48,2560]{2,0,1:T(8,128)(2,1)S(1)} %bitcast.24) | data formatting | bytes 15728640 | tf_op jit(solution)/shard_map/reshape | solution.py:36
  114.9 100.3 %all_to_all.16 = bf16[32,48,2560]{2,1,0:T(8,128)(2,1)S(1)} all-to-all(bf16[32,48,2560]{2,1,0:T(8,128)(2,1)} %copy.15), channel_id=1, replica_groups=mesh['expert'=32,'etp'=4] {'expert'}, dimensions={0} | all-to-all | bytes 15728640 | tf_op jit(solution)/shard_map/all_to_all | solution.py:39
  215.2 3.1 copy-done.2
  218.2 10.1 %fusion.1 = f32[1536,1024]{1,0:T(8,128)} fusion(bf16[1536,2560]{1,0:T(8,128)(2,1)S(1)} %bitcast.25, bf16[1,2560,1024]{2,1,0:T(8,128)(2,1)S(1)} %bitcast.31), kind=kOutput, calls=%fused_computation.3 | convolution fusion | flops 8053063680 | bytes 19398656 | tf_op jit(solution)/shard_map/dot_general | solution.py:10
  228.4 25.3 %convolution_convert_fusion = bf16[1536,2560]{1,0:T(8,128)(2,1)} fusion(bf16[1,1024,2560]{2,1,0:T(8,128)(2,1)} %param.11, f32[1536,1024]{1,0:T(8,128)} %fusion.1, bf16[1536,2560]{1,0:T(8,128)(2,1)} %bitcast.26, bf16[1,2560,1024]{2,1,0:T(8,128)(2,1)} %param.9), kind=kOutput, calls=%fused_computation | convolution fusion | flops 16119496704 | bytes 32505856 | tf_op jit(solution)/shard_map/dot_general | solution.py:41
  253.7 95.1 %all_to_all.17 = bf16[32,48,2560]{2,1,0:T(8,128)(2,1)S(1)} all-to-all(bf16[32,48,2560]{2,1,0:T(8,128)(2,1)} %bitcast.27), channel_id=1, replica_groups=mesh['expert'=32,'etp'=4] {'expert'}, dimensions={0} | all-to-all | bytes 15728640 | tf_op jit(solution)/shard_map/all_to_all | solution.py:47
  348.8 7.4 %copy.16 = bf16[32,48,2560]{2,0,1:T(8,128)(2,1)} copy(bf16[32,48,2560]{2,1,0:T(8,128)(2,1)S(1)} %all_to_all.17) | data formatting | bytes 15728640 | tf_op jit(solution)/shard_map/all_to_all | solution.py:47
  356.1 0.0 reduce-scatter.2.cloned.1.call-update
  356.2 0.0 copy-start.3
  356.2 0.0 copy-start.1
  356.2 73.7 %reduce-scatter.2.cloned.1.call-done = bf16[32,12,2560]{2,0,1:T(8,128)(2,1)} async-done(((bf16[32,48,2560]{2,0,1:T(8,128)(2,1)}), bf16[32,12,2560]{2,0,1:T(8,128)(2,1)}) %reduce-scatter.2.cloned.1.call-update) | async-done | bytes 1966096 | tf_op jit(solution)/shard_map/reduce_scatter | solution.py:48
  429.9 2.7 copy.17
  432.5 2.0 reshape.30
  434.6 2.9 fusion.9
  (10 shorter events, 0.0 us)
Async XLA Ops:
  6.5 2.5 copy-start
  6.5 423.3 %reduce-scatter.2.cloned.1.call-start = ((), (), s32[]{:S(2)}) async-start(), calls=%async_computation.4 | async-start | bytes 9830400 | tf_op jit(solution)/shard_map/reduce_scatter | solution.py:48
  107.5 110.7 %slice-start = ((s8[5242880]{0:T(1024)(128)(4,1)}), s8[1048576]{0:T(1024)(128)(4,1)S(1)}, s32[]{:S(2)}) async-start(s8[5242880]{0:T(1024)(128)(4,1)} %bitcast.30), calls=%async_computation.5 | async-start | bytes 2097152
  114.9 103.3 %slice-start.1 = ((s8[5242880]{0:T(1024)(128)(4,1)}), s8[4194304]{0:T(1024)(128)(4,1)S(1)}, s32[]{:S(2)}) async-start(s8[5242880]{0:T(1024)(128)(4,1)} %bitcast.30), calls=%async_computation.6 | async-start | bytes 8388608
  215.2 3.1 copy-start.2
  356.2 78.4 %copy-start.3 = (f32[128]{0:T(128)S(1)}, f32[128]{0:T(128)}, u32[]{:S(2)}) copy-start(f32[128]{0:T(128)} %param.8) | copy-start | bytes 1540
  356.2 81.3 %copy-start.1 = (bf16[128,2560]{1,0:T(8,128)(2,1)S(1)}, bf16[128,2560]{1,0:T(8,128)(2,1)}, u32[]{:S(2)}) copy-start(bf16[128,2560]{1,0:T(8,128)(2,1)} %param.6) | copy-start | bytes 1966084
Sparse Core Ops, SparseCore 0:
  356.3 73.5 reduce-scatter.1
